TPU v7x, 32 devices: a whole 2x2x4 slice. The times are simulated.
32 devices in a mesh: dp: 16 (over z, x, core), opt: 2 (over y).
Axes of the slice: x: 2, y: 2, z: 4, core: 2. Of those that a mesh axis runs over, the one named last changes fastest.
Arguments:
- params: bfloat16 [12595200], P('opt'), may hold values from -2 to 2, as said below
- moment_one: float32 [12595200], P('opt'), may hold values from -160 to 160
- moment_two: float32 [12595200], P('opt'), may hold values from 81.92 to 8192
- inputs: bfloat16 [64, 128, 1024], P(('dp', 'opt')), may hold values from -6 to 6
- cotangent: bfloat16 [64, 128, 1024], P(('dp', 'opt')), may hold values from -6 to 6
- segments: int32 [64, 128], P(('dp', 'opt')), may hold values from 0 to 3, never falling along the last dimension, each value on 1 to 64 neighbouring positions
- windows: int32 [64], P(('dp', 'opt')), may hold values from 128 to 512, as said below
Outputs:
- output: bfloat16 [64, 128, 1024], P(('dp', 'opt'))
- input_grad: bfloat16 [64, 128, 1024], P(('dp', 'opt'))
- grads: float32 [12595200], P('opt')
- new_params: float32 [12595200], P('opt')
- new_moment_one: float32 [12595200], P('opt')
- new_moment_two: float32 [12595200], P('opt')
- new_copy: bfloat16 [12595200], P('opt')
Inputs may be any that keep to these rules, and one draw needn't show every extreme that they name: `params`: the flat parameter vector in the layout of the steps; gains near 1. `windows`: every draw holds a sequence with window 512 and one with window 512 // 4.
All inputs are finite; a program needn't handle non-finite values.
Results may differ from a plain program's by a relative error of at most 0.0094.
Values may be sent and summed in bfloat16 or wider, within the bound.
No kernel may reach another device: no remote copies, remote signals or barrier semaphores. Data moves between devices by JAX's collectives and lax.ppermute only.
A program may use at most 448 MiB of HBM per device.

v0:
```python
import math
import jax
import jax.numpy as jnp
from jax import lax
from jax.sharding import PartitionSpec as P

HEADS = 16
HEAD_DIM = 64
FF = 4096
MATRIX_PARAMS = 12582912
GELU_C = math.sqrt(2.0 / math.pi)
LEARN_RATE = 0.01
WEIGHT_DECAY = 0.1


def unpack_weights(flat_values, model_width, hidden_units):
    layout = [
        (model_width, 3 * model_width),
        (model_width, model_width),
        (model_width, hidden_units),
        (hidden_units, model_width),
    ]
    layout = layout + [(model_width,)] * 7 + [(hidden_units,), (model_width,)]
    pieces = []
    position = 0
    for piece_dims in layout:
        amount = math.prod(piece_dims)
        pieces.append(flat_values[position : position + amount].reshape(piece_dims))
        position = position + amount
    return pieces


def standardize(values):
    centred = values - jnp.mean(values, axis=-1, keepdims=True)
    inverse = lax.rsqrt(jnp.mean(centred * centred, axis=-1, keepdims=True) + 1e-05)
    return (centred * inverse, inverse)


def gelu_value(values):
    return 0.5 * values * (1.0 + jnp.tanh(GELU_C * (values + 0.044715 * values * values * values)))


def gelu_slope(values):
    tangent = jnp.tanh(GELU_C * (values + 0.044715 * values * values * values))
    return 0.5 * (1.0 + tangent) + 0.5 * values * (1.0 - tangent * tangent) * GELU_C * (
        1.0 + 0.134145 * values * values
    )


def norm_back(grad_norm, normed, inverse):
    return inverse * (
        grad_norm
        - jnp.mean(grad_norm, axis=-1, keepdims=True)
        - normed * jnp.mean(grad_norm * normed, axis=-1, keepdims=True)
    )


def column_sum(values):
    return jnp.sum(values.astype(jnp.float32), axis=0)


def inner_rows(left_rows, right_rows):
    return lax.dot_general(
        left_rows, right_rows, (((0,), (0,)), ((), ())), preferred_element_type=jnp.float32
    )


def sequence_pass(weights, tokens, cotangent_rows, segment_ids, window_len):
    (
        qkv_weight,
        out_weight,
        fc_weight,
        proj_weight,
        first_gain,
        first_shift,
        query_bias,
        value_bias,
        out_bias,
        second_gain,
        second_shift,
        fc_bias,
        proj_bias,
    ) = weights
    seq_rows, model_width = tokens.shape
    score_scale = 1.0 / math.sqrt(HEAD_DIM)
    first_gain_f = first_gain.astype(jnp.float32)
    second_gain_f = second_gain.astype(jnp.float32)
    residual_in = tokens.astype(jnp.float32)
    normed_one, inverse_one = standardize(residual_in)
    hidden_one = (normed_one * first_gain_f + first_shift.astype(jnp.float32)).astype(jnp.bfloat16)
    qkv_bias = jnp.concatenate([query_bias, jnp.zeros_like(query_bias), value_bias]).astype(
        jnp.float32
    )
    projected = (
        jnp.dot(hidden_one, qkv_weight, preferred_element_type=jnp.float32) + qkv_bias
    ).astype(jnp.bfloat16)
    queries = projected[:, :model_width].reshape(seq_rows, HEADS, HEAD_DIM)
    key_heads = projected[:, model_width : 2 * model_width].reshape(seq_rows, HEADS, HEAD_DIM)
    value_heads = projected[:, 2 * model_width :].reshape(seq_rows, HEADS, HEAD_DIM)
    positions = jnp.arange(seq_rows)
    allowed = (
        (positions[None, :] <= positions[:, None])
        & (positions[:, None] - positions[None, :] < window_len)
        & (segment_ids[:, None] == segment_ids[None, :])
    )

    def masked_scores():
        raw_scores = (
            jnp.einsum("qhd,khd->hqk", queries, key_heads, preferred_element_type=jnp.float32)
            * score_scale
        )
        return jnp.where(allowed[None], raw_scores, -jnp.inf)

    scores = masked_scores()
    row_max = jnp.max(scores, axis=-1, keepdims=True)
    log_total = row_max + jnp.log(jnp.sum(jnp.exp(scores - row_max), axis=-1, keepdims=True))
    probs = jnp.exp(scores - log_total).astype(jnp.bfloat16)
    mixed = jnp.einsum("hqk,khd->qhd", probs, value_heads, preferred_element_type=jnp.float32)
    mixed = mixed.reshape(seq_rows, model_width).astype(jnp.bfloat16)
    attended = jnp.dot(mixed, out_weight, preferred_element_type=jnp.float32) + out_bias.astype(
        jnp.float32
    )
    residual_mid = residual_in + attended
    normed_two, inverse_two = standardize(residual_mid)
    hidden_two = (normed_two * second_gain_f + second_shift.astype(jnp.float32)).astype(
        jnp.bfloat16
    )
    before_act = jnp.dot(
        hidden_two, fc_weight, preferred_element_type=jnp.float32
    ) + fc_bias.astype(jnp.float32)
    activated = gelu_value(before_act).astype(jnp.bfloat16)
    result_rows = jnp.dot(
        activated, proj_weight, preferred_element_type=jnp.float32
    ) + proj_bias.astype(jnp.float32)
    output_rows = (residual_mid + result_rows).astype(jnp.bfloat16)
    grad_proj = inner_rows(activated, cotangent_rows)
    grad_proj_bias = column_sum(cotangent_rows)
    grad_act = jnp.dot(cotangent_rows, proj_weight.T, preferred_element_type=jnp.float32)
    grad_before = (grad_act * gelu_slope(before_act)).astype(jnp.bfloat16)
    grad_fc = inner_rows(hidden_two, grad_before)
    grad_fc_bias = column_sum(grad_before)
    grad_hidden_two = jnp.dot(grad_before, fc_weight.T, preferred_element_type=jnp.float32)
    grad_second_gain = jnp.sum(grad_hidden_two * normed_two, axis=0)
    grad_second_shift = jnp.sum(grad_hidden_two, axis=0)
    grad_mid = cotangent_rows.astype(jnp.float32) + norm_back(
        grad_hidden_two * second_gain_f, normed_two, inverse_two
    )
    grad_attended = grad_mid.astype(jnp.bfloat16)
    grad_out = inner_rows(mixed, grad_attended)
    grad_out_bias = column_sum(grad_attended)
    grad_mixed = jnp.dot(grad_attended, out_weight.T, preferred_element_type=jnp.float32).astype(
        jnp.bfloat16
    )
    grad_mixed = grad_mixed.reshape(seq_rows, HEADS, HEAD_DIM)
    grad_probs = jnp.einsum(
        "qhd,khd->hqk", grad_mixed, value_heads, preferred_element_type=jnp.float32
    )
    exact_probs = jnp.exp(masked_scores() - log_total)
    row_terms = jnp.sum(exact_probs * grad_probs, axis=-1, keepdims=True)
    grad_scores = (exact_probs * (grad_probs - row_terms)).astype(jnp.bfloat16)
    grad_queries = (
        jnp.einsum("hqk,khd->qhd", grad_scores, key_heads, preferred_element_type=jnp.float32)
        * score_scale
    )
    grad_keys = (
        jnp.einsum("hqk,qhd->khd", grad_scores, queries, preferred_element_type=jnp.float32)
        * score_scale
    )
    grad_values = jnp.einsum("hqk,qhd->khd", probs, grad_mixed, preferred_element_type=jnp.float32)
    grad_projected = jnp.concatenate(
        [
            grad_queries.reshape(seq_rows, model_width),
            grad_keys.reshape(seq_rows, model_width),
            grad_values.reshape(seq_rows, model_width),
        ],
        axis=1,
    ).astype(jnp.bfloat16)
    grad_qkv = inner_rows(hidden_one, grad_projected)
    grad_query_bias = column_sum(grad_projected[:, :model_width])
    grad_value_bias = column_sum(grad_projected[:, 2 * model_width :])
    grad_hidden_one = jnp.dot(grad_projected, qkv_weight.T, preferred_element_type=jnp.float32)
    grad_first_gain = jnp.sum(grad_hidden_one * normed_one, axis=0)
    grad_first_shift = jnp.sum(grad_hidden_one, axis=0)
    grad_input = (
        grad_mid + norm_back(grad_hidden_one * first_gain_f, normed_one, inverse_one)
    ).astype(jnp.bfloat16)
    weight_grads = [
        grad_qkv,
        grad_out,
        grad_fc,
        grad_proj,
        grad_first_gain,
        grad_first_shift,
        grad_query_bias,
        grad_value_bias,
        grad_out_bias,
        grad_second_gain,
        grad_second_shift,
        grad_fc_bias,
        grad_proj_bias,
    ]
    return (output_rows, grad_input, weight_grads)


def body(params, moment_one, moment_two, inputs, cotangent, segments, windows):
    gathered = lax.all_gather(params, "opt", axis=0, tiled=True)
    weights = unpack_weights(gathered, inputs.shape[2], FF)
    output_list = []
    input_list = []
    totals = None
    for micro_index in range(inputs.shape[0]):
        output_rows, grad_rows, weight_grads = sequence_pass(
            weights,
            inputs[micro_index],
            cotangent[micro_index],
            segments[micro_index],
            windows[micro_index],
        )
        output_list.append(output_rows)
        input_list.append(grad_rows)
        if totals is None:
            totals = weight_grads
        else:
            totals = [
                earlier_sum + later_sum for earlier_sum, later_sum in zip(totals, weight_grads)
            ]
    flat_total = jnp.concatenate([piece.reshape(-1) for piece in totals])
    opt_count = lax.axis_size("opt")
    dp_count = lax.axis_size("dp")
    blocks = (
        flat_total.reshape(opt_count, dp_count, -1)
        .transpose(1, 0, 2)
        .reshape(opt_count * dp_count, -1)
    )
    owned_piece = lax.psum_scatter(blocks, ("dp", "opt"), scatter_dimension=0, tiled=True)
    owned_grads = lax.all_gather(owned_piece, "dp", axis=0, tiled=True).reshape(-1)
    shard_length = params.shape[0]
    positions = lax.axis_index("opt") * shard_length + jnp.arange(shard_length, dtype=jnp.int32)
    decay_mask = (positions < MATRIX_PARAMS).astype(jnp.float32)
    old_values = params.astype(jnp.float32)
    first_moment = 0.5 * moment_one + 0.5 * owned_grads
    second_moment = 0.5 * moment_two + 0.5 * owned_grads * owned_grads
    update = (
        first_moment / (jnp.sqrt(second_moment) + 1e-08) + WEIGHT_DECAY * decay_mask * old_values
    )
    new_values = old_values - LEARN_RATE * update
    return (
        jnp.stack(output_list),
        jnp.stack(input_list),
        owned_grads,
        new_values,
        first_moment,
        second_moment,
        new_values.astype(jnp.bfloat16),
    )


def solution(mesh):
    placed = (
        P("opt"),
        P("opt"),
        P("opt"),
        P(("dp", "opt"), None, None),
        P(("dp", "opt"), None, None),
        P(("dp", "opt"), None),
        P(("dp", "opt")),
    )
    return jax.shard_map(
        body,
        mesh=mesh,
        in_specs=placed,
        out_specs=(
            P(("dp", "opt"), None, None),
            P(("dp", "opt"), None, None),
            P("opt"),
            P("opt"),
            P("opt"),
            P("opt"),
            P("opt"),
        ),
        check_vma=False,
    )
```

profile of v0, /device:TPU:0, one launch (start us, length us, event | category | flops | bytes accessed | tf_op | source)
XLA Modules:
  0.0 1707.5 jit_solution(409223282035159766)
XLA Ops:
  9.1 1.4 fusion.87
  10.5 298.3 %all-gather.4.cloned.1.call-done = bf16[12595200]{0:T(1024)(128)(2,1)} async-done(((bf16[6297600]{0:T(1024)(128)(2,1)}), bf16[12595200]{0:T(1024)(128)(2,1)}) %all-gather.4.cloned.1.call-update) | async-done | bytes 25190416 | tf_op jit(solution)/shard_map/all_gather | solution.py:206
  308.8 6.4 slice.158
  315.2 10.3 slice.129
  325.5 1.3 slice_convert_fusion.3
  326.8 3.9 fusion.6
  332.0 3.0 slice.164
  335.0 2.8 slice.138
  337.9 11.4 fusion.105
  349.3 13.3 slice.146
  362.5 13.3 slice.143
  376.1 1.6 fusion.110
  378.7 3.9 fusion.5
  382.6 0.8 fusion.106
  383.5 0.8 copy.71
  384.3 1.1 copy.72
  385.4 1.9 copy.73
  387.3 1.4 fusion.111
  390.1 1.0 slice_convert_fusion
  391.1 5.0 convolution_add_fusion
  396.1 1.3 convolution_add_fusion.1
  397.5 1.8 slice-done.7
  399.3 6.6 convert_reduce_fusion
  405.9 4.2 fusion.113
  410.1 4.3 convert_reduce_fusion.1
  414.5 3.1 multiply_reduce_fusion.3
  417.7 2.0 convert_reduce_fusion.2
  419.6 0.8 copy-done.20
  420.4 0.8 convolution_convert_fusion.1
  421.2 0.8 copy.83
  422.1 1.4 convolution_convert_fusion
  423.5 1.4 multiply_reduce_fusion
  425.2 1.2 fusion.28
  426.4 1.0 fusion.27
  427.4 1.6 convolution_convert_fusion.3
  429.0 1.2 copy.79
  433.8 8.6 fusion.102
  442.4 8.8 fusion.72
  454.2 2.2 fusion.65
  456.4 2.0 fusion.66
  458.4 3.8 fusion.63
  462.2 6.8 add_bitcast_fusion.2
  468.9 12.3 copy.96
  481.3 10.5 constant_dynamic-update-slice_fusion.11
  492.5 3.0 copy.97
  495.5 14.6 add_bitcast_fusion.1
  510.1 14.8 copy.98
  525.0 8.6 add_bitcast_fusion
  533.6 9.8 copy.99
  543.4 4.4 constant_dynamic-update-slice_fusion.10
  547.8 6.0 constant_dynamic-update-slice_fusion.9
  553.9 6.0 constant_dynamic-update-slice_fusion.8
  565.3 51.0 %reshape.377 = f32[2,16,393600]{2,1,0:T(8,128)} reshape(f32[12595200]{0:T(1024)} %constant_dynamic-update-slice_fusion) | data formatting | bytes 100761600 | tf_op jit(solution)/shard_map/reshape | solution.py:231
  616.2 68.9 %copy.87 = f32[16,2,393600]{2,1,0:T(2,128)} copy(f32[16,2,393600]{2,0,1:T(8,128)} %bitcast.212) | data formatting | bytes 100761600 | tf_op jit(solution)/shard_map/transpose | solution.py:232
  685.2 78.3 %reshape.378 = f32[32,393600]{1,0:T(8,128)} reshape(f32[16,2,393600]{2,1,0:T(2,128)} %copy.87) | data formatting | bytes 100761600 | tf_op jit(solution)/shard_map/reshape | solution.py:233
  763.6 721.8 %all-reduce.3.cloned.1.call-done = f32[32,393600]{1,0:T(8,128)} async-done(((f32[32,393600]{1,0:T(8,128)}), f32[32,393600]{1,0:T(8,128)}) %all-reduce.3.cloned.1.call-update) | async-done | bytes 50380816
  1485.4 6.6 dynamic-slice_bitcast_fusion
  1492.0 5.1 fusion.29
  1497.3 6.2 fusion.30
  1503.5 0.8 pad_maximum_fusion.2
  1504.9 0.8 pad_maximum_fusion.3
  1505.8 114.9 %all-gather.6.cloned.1.call-done = f32[16,1,393600]{2,1,0:T(1,128)} async-done(((f32[1,1,393600]{2,1,0:T(1,128)}), f32[16,1,393600]{2,1,0:T(1,128)}) %all-gather.6.cloned.1.call-update) | async-done | bytes 25190416 | tf_op jit(solution)/shard_map/all_gather | solution.py:236
  1620.7 61.1 %fusion.103 = (bf16[6297600]{0:T(1024)(128)(2,1)}, f32[6297600]{0:T(1024)}, f32[6297600]{0:T(1024)}, f32[6297600]{0:T(1024)}) fusion(s32[]{:T(128)S(6)} %mul.433, bf16[6297600]{0:T(1024)(128)(2,1)} %param.7, f32[6297600]{0:T(1024)} %bitcast.215, f32[6297600]{0:T(1024)} %param.9, f32[6297600]{0:T(1024)} %param.8), kind=kLoop, calls=%fused_computation.218 | loop fusion | flops 107059200 | bytes 176332800 | tf_op jit(solution)/shard_map/convert_element_type | solution.py:254
  1681.8 19.0 %copy.114 = f32[6297600]{0:T(1024)} copy(f32[6297600]{0:T(1024)} %bitcast.216) | data formatting | bytes 50380800
  (247 shorter events, 19.2 us)
Async XLA Ops:
  7.2 301.6 %all-gather.4.cloned.1.call-start = ((), (), s32[]{:S(2)}) async-start(), calls=%async_computation | async-start | bytes 37785600 | tf_op jit(solution)/shard_map/all_gather | solution.py:206
  7.9 1477.5 %all-reduce.3.cloned.1.call-start = ((), (), s32[]{:S(2)}) async-start(), calls=%async_computation.2 | async-start | bytes 100761600
  8.7 449.6 %copy-start.64 = (f32[128]{0:T(128)}, f32[128]{0:T(128)S(1)}, u32[]{:S(2)}) copy-start(f32[128]{0:T(128)S(1)} %get-tuple-element.90) | copy-start | bytes 1540
  8.7 453.4 %copy-start.62 = (f32[128]{0:T(128)}, f32[128]{0:T(128)S(1)}, u32[]{:S(2)}) copy-start(f32[128]{0:T(128)S(1)} %get-tuple-element.89) | copy-start | bytes 1540
  9.0 453.1 %copy-start.66 = (f32[128]{0:T(128)}, f32[128]{0:T(128)S(1)}, u32[]{:S(2)}) copy-start(f32[128]{0:T(128)S(1)} %add_rsqrt_fusion.1) | copy-start | bytes 1540
  9.1 449.3 %copy-start.68 = (f32[128]{0:T(128)}, f32[128]{0:T(128)S(1)}, u32[]{:S(2)}) copy-start(f32[128]{0:T(128)S(1)} %add_rsqrt_fusion.3) | copy-start | bytes 1540
  326.8 135.4 %copy-start.52 = (f32[1024]{0:T(1024)}, f32[1024]{0:T(1024)S(1)}, u32[]{:S(2)}) copy-start(f32[1024]{0:T(1024)S(1)} %get-tuple-element.46) | copy-start | bytes 12292
  330.9 44.9 %copy-start.34 = (bf16[128,1024]{0,1:T(8,128)(2,1)}, bf16[128,1024]{0,1:T(8,128)(2,1)S(1)}, u32[]{:S(2)}) copy-start(bf16[128,1024]{0,1:T(8,128)(2,1)S(1)} %copy.75) | copy-start | bytes 786436
  385.4 3.8 copy-start.35
  389.8 27.8 %copy-start.7 = (f32[128,1024]{1,0:T(8,128)}, f32[128,1024]{1,0:T(8,128)S(1)}, u32[]{:S(2)}) copy-start(f32[128,1024]{1,0:T(8,128)S(1)} %get-tuple-element.78) | copy-start | bytes 1572868
  389.9 6.2 slice-start
  391.1 5.1 slice-start.1
  391.1 6.4 slice-start.6
  396.1 3.2 slice-start.7
  399.3 10.8 copy-start.17
  405.9 4.2 copy-start.44
  414.5 3.2 copy-start.45
  426.4 3.7 copy-start.2
  433.8 8.6 copy-start.18
  433.8 8.6 copy-start.46
  433.8 20.4 %slice-start.8 = ((s8[6291456]{0:T(1024)(128)(4,1)}), s8[4194304]{0:T(1024)(128)(4,1)S(1)}, s32[]{:S(2)}) async-start(s8[6291456]{0:T(1024)(128)(4,1)} %bitcast.223), calls=%async_computation.11 | async-start | bytes 8388608
  442.4 9.5 copy-start.29
  442.4 11.7 slice-start.9
  442.4 11.7 copy-start.48
  481.3 10.5 copy-start.21
  481.3 10.5 copy-start.41
  495.5 29.4 %slice-start.2 = ((s8[16777216]{0:T(1024)(128)(4,1)}), s8[4194304]{0:T(1024)(128)(4,1)S(1)}, s32[]{:S(2)}) async-start(s8[16777216]{0:T(1024)(128)(4,1)} %bitcast.213), calls=%async_computation.5 | async-start | bytes 8388608
  495.5 29.4 %slice-start.3 = ((s8[16777216]{0:T(1024)(128)(4,1)}), s8[4194304]{0:T(1024)(128)(4,1)S(1)}, s32[]{:S(2)}) async-start(s8[16777216]{0:T(1024)(128)(4,1)} %bitcast.213), calls=%async_computation.6 | async-start | bytes 8388608
  495.5 29.4 %slice-start.4 = ((s8[16777216]{0:T(1024)(128)(4,1)}), s8[4194304]{0:T(1024)(128)(4,1)S(1)}, s32[]{:S(2)}) async-start(s8[16777216]{0:T(1024)(128)(4,1)} %bitcast.213), calls=%async_computation.7 | async-start | bytes 8388608
  510.1 14.8 slice-start.5
  510.1 14.8 copy-start.11
  510.1 14.9 copy-start.47
  533.6 14.2 copy-start
  553.8 6.1 copy-start.72
  553.8 6.1 copy-start.73
  553.8 6.7 copy-start.70
  553.8 6.7 copy-start.71
  553.8 7.3 copy-start.58
  553.8 7.3 copy-start.59
  553.8 7.9 copy-start.56
  553.8 7.8 copy-start.57
  553.9 8.4 copy-start.54
  553.9 8.4 copy-start.55
  553.9 10.2 copy-start.60
  553.9 10.2 copy-start.61
  763.5 857.2 %all-gather.6.cloned.1.call-start = ((), (), s32[]{:S(2)}) async-start(), calls=%async_computation.1 | async-start | bytes 26764800 | tf_op jit(solution)/shard_map/all_gather | solution.py:236
  763.6 728.5 %copy-start.6 = (f32[128,1024]{1,0:T(8,128)S(1)}, f32[128,1024]{1,0:T(8,128)}, u32[]{:S(2)}) copy-start(f32[128,1024]{1,0:T(8,128)} %copy-done.3) | copy-start | bytes 1572868
  763.6 728.5 %copy-start.74 = (f32[1024]{0:T(1024)S(1)}, f32[1024]{0:T(1024)}, u32[]{:S(2)}) copy-start(f32[1024]{0:T(1024)} %get-tuple-element.40) | copy-start | bytes 12292
  1492.0 5.2 copy-start.9
  1492.0 5.2 copy-start.19
  1497.2 7.2 copy-start.80
  1497.2 7.2 copy-start.79
  1497.2 7.2 copy-start.78
  1497.2 7.2 copy-start.77
  1497.2 7.2 copy-start.16
  1497.3 7.2 copy-start.22
  1497.3 7.2 copy-start.25
  1497.3 7.2 copy-start.50
  1497.3 7.2 copy-start.51
  1497.3 7.2 copy-start.53
  1497.3 7.2 copy-start.63
  1497.3 7.2 copy-start.65
  1497.3 7.2 copy-start.67
  1497.3 7.2 copy-start.69
  (30 other events, 49.8 us)
Sparse Core Ops, SparseCore 0:
  9.6 299.1 all-gather.3
  763.6 721.7 all-reduce.2
  1492.1 128.5 all-gather.5
where the time goes:
time: 1720 us; the launch traced here: 1710 us
  waiting for transfers between devices  1140 us (66%)
  local copies, waits for them, and re-layouts  364 us (21%)
  matrix products  114 us (7%)
  other arithmetic  78.9 us (5%)
    unnamed x4, waiting for transfers between devices  723 us
    all_gather x1, waiting for transfers between devices, body(): gathered = lax.all_gather(params, 'opt', axis=0, tiled=True)  298 us
    all_gather x1, waiting for transfers between devices, body(): lax.all_gather(owned_piece, 'dp', axis=0, tiled=True).reshape(-1)  115 us
    unnamed x192, local copies, waits for them, and re-layouts  97.4 us
    reshape x1, local copies, waits for them, and re-layouts, body(): blocks = flat_total.reshape(opt_count, dp_count, -1).transpose(1, 0, 2).r...  78.3 us
    transpose x1, local copies, waits for them, and re-layouts, body(): blocks = flat_total.reshape(opt_count, dp_count, -1).transpose(1, 0, 2).r...  68.9 us
    convert_element_type x1, other arithmetic, body(): new_values.astype(jnp.bfloat16)  61.1 us
    slice x7, local copies, waits for them, and re-layouts, unpack_weights(): pieces.append(flat_values[position:position + amount].reshape(piece_dims))  60.5 us
  transfers between devices with their start and end apart: 3, of which 3 were waited for; matrix products, arithmetic and copies ran while one was open for 1% of the time, Pallas kernels for 0%

commit v1 on v0

--- a/solution.py
+++ b/solution.py
@@ -11,6 +11,24 @@
 GELU_C = math.sqrt(2.0 / math.pi)
 LEARN_RATE = 0.01
 WEIGHT_DECAY = 0.1
+
+
+def collect(shard, axis, dim):
+    ways, here, step = (lax.axis_size(axis), lax.axis_index(axis), shard.shape[dim])
+    shape = [n * ways if d == dim else n for d, n in enumerate(shard.shape)]
+    full = lax.dynamic_update_slice_in_dim(
+        jnp.zeros(shape, shard.dtype), shard, here * step, axis=dim
+    )
+    going_up = going_down = shard
+    for far in range(1, ways // 2 + 1):
+        going_up = lax.ppermute(going_up, axis, [(d, (d + 1) % ways) for d in range(ways)])
+        full = lax.dynamic_update_slice_in_dim(full, going_up, (here - far) % ways * step, axis=dim)
+        if 2 * far < ways:
+            going_down = lax.ppermute(going_down, axis, [(d, (d - 1) % ways) for d in range(ways)])
+            full = lax.dynamic_update_slice_in_dim(
+                full, going_down, (here + far) % ways * step, axis=dim
+            )
+    return full
 
 
 def unpack_weights(flat_values, model_width, hidden_units):
@@ -233,7 +251,7 @@
         .reshape(opt_count * dp_count, -1)
     )
     owned_piece = lax.psum_scatter(blocks, ("dp", "opt"), scatter_dimension=0, tiled=True)
-    owned_grads = lax.all_gather(owned_piece, "dp", axis=0, tiled=True).reshape(-1)
+    owned_grads = collect(owned_piece, "dp", 0).reshape(-1)
     shard_length = params.shape[0]
     positions = lax.axis_index("opt") * shard_length + jnp.arange(shard_length, dtype=jnp.int32)
     decay_mask = (positions < MATRIX_PARAMS).astype(jnp.float32)

time: 1720 us -> 2370 us (1.38)
  local copies, waits for them, and re-layouts: 364 us -> 863 us
  starting transfers between devices: 0.12 us -> 208 us
  waiting for transfers between devices: 1140 us -> 1060 us
    dynamic_update_slice x0 -> x16, local copies, waits for them, and re-layouts: none -> 486 us  [the longest x8 243 us: collect(): lax.dynamic_update_slice_in_dim(full, going_up, (here - far) % ways * ste...]
    ppermute x0 -> x15, starting transfers between devices: none -> 208 us  [the longest x8 204 us: collect(): lax.ppermute(going_up, axis, [(d, (d + 1) % ways) for d in range(ways)])]
    all_gather x1 -> x0, waiting for transfers between devices: 115 us -> none  [body(): lax.all_gather(owned_piece, 'dp', axis=0, tiled=True).reshape(-1)]
    ppermute x0 -> x15, waiting for transfers between devices: none -> 41 us  [the longest x8 41 us: collect(): lax.ppermute(going_up, axis, [(d, (d + 1) % ways) for d in range(ways)])]
    unnamed x192 -> x259, local copies, waits for them, and re-layouts: 97.4 us -> 78.8 us
    unnamed x4 -> x3, waiting for transfers between devices: 723 us -> 723 us
  transfers between devices with their start and end apart: 3 -> 17, of which waited for: 3 -> 9; matrix products, arithmetic and copies ran while one was open for 1% -> 20% of each run, Pallas kernels for 0% -> 0%
where the time goes in v1:
time: 2370 us; the launch traced here: 2350 us
  waiting for transfers between devices  1060 us (45%)
  local copies, waits for them, and re-layouts  863 us (36%)
  starting transfers between devices  208 us (9%)
  matrix products  115 us (5%)
  other arithmetic  82 us (3%)
    unnamed x3, waiting for transfers between devices  723 us
    all_gather x1, waiting for transfers between devices, body(): gathered = lax.all_gather(params, 'opt', axis=0, tiled=True)  298 us
    dynamic_update_slice x8, local copies, waits for them, and re-layouts, collect(): lax.dynamic_update_slice_in_dim(full, going_up, (here - far) % ways * ste...  243 us
    dynamic_update_slice x7, local copies, waits for them, and re-layouts, collect(): lax.dynamic_update_slice_in_dim(full, going_down, (here + far) % ways * s...  213 us
    ppermute x8, starting transfers between devices, collect(): lax.ppermute(going_up, axis, [(d, (d + 1) % ways) for d in range(ways)])  204 us
    unnamed x259, local copies, waits for them, and re-layouts  78.8 us
    reshape x1, local copies, waits for them, and re-layouts, body(): blocks = flat_total.reshape(opt_count, dp_count, -1).transpose(1, 0, 2).r...  78.7 us
    transpose x1, local copies, waits for them, and re-layouts, body(): blocks = flat_total.reshape(opt_count, dp_count, -1).transpose(1, 0, 2).r...  68.9 us
  transfers between devices with their start and end apart: 17, of which 9 were waited for; matrix products, arithmetic and copies ran while one was open for 20% of the time, Pallas kernels for 0%

profile of v1, /device:TPU:0, one launch (start us, length us, event | category | flops | bytes accessed | tf_op | source)
XLA Modules:
  0.0 2345.1 jit_solution(2070826129808236557)
XLA Ops:
  10.5 298.3 %all-gather.2.cloned.1.call-done = bf16[12595200]{0:T(1024)(128)(2,1)} async-done(((bf16[6297600]{0:T(1024)(128)(2,1)}), bf16[12595200]{0:T(1024)(128)(2,1)}) %all-gather.2.cloned.1.call-update) | async-done | bytes 25190416 | tf_op jit(solution)/shard_map/all_gather | solution.py:224
  308.8 6.4 slice.158
  315.2 10.3 slice.129
  326.8 3.9 fusion.5
  332.5 3.0 slice.164
  342.3 11.4 fusion.105
  353.7 13.3 slice.143
  366.9 13.3 slice.146
  380.9 5.0 convolution_add_fusion.1
  386.9 4.3 convert_reduce_fusion.1
  391.2 8.6 fusion.102
  413.4 4.9 convolution_add_fusion
  418.3 4.3 convert_reduce_fusion
  425.6 3.1 multiply_reduce_fusion.3
  448.2 9.3 fusion.72
  457.5 9.1 add_bitcast_fusion.1
  466.6 14.3 copy.98
  481.7 3.0 copy.97
  489.9 3.0 fusion.65
  493.0 6.7 add_bitcast_fusion.2
  499.7 12.3 copy.96
  512.1 10.4 constant_dynamic-update-slice_fusion.11
  522.5 8.3 add_bitcast_fusion
  530.9 9.5 copy.99
  540.4 6.7 fusion.63
  549.6 8.4 constant_dynamic-update-slice_fusion.9
  560.6 6.1 constant_dynamic-update-slice_fusion.8
  572.1 50.8 %reshape.377 = f32[2,16,393600]{2,1,0:T(8,128)} reshape(f32[12595200]{0:T(1024)} %constant_dynamic-update-slice_fusion) | data formatting | bytes 100761600 | tf_op jit(solution)/shard_map/reshape | solution.py:249
  622.9 68.9 %copy.87 = f32[16,2,393600]{2,1,0:T(2,128)} copy(f32[16,2,393600]{2,0,1:T(8,128)} %bitcast.209) | data formatting | bytes 100761600 | tf_op jit(solution)/shard_map/transpose | solution.py:250
  691.8 78.7 %reshape.378 = f32[32,393600]{1,0:T(8,128)} reshape(f32[16,2,393600]{2,1,0:T(2,128)} %copy.87) | data formatting | bytes 100761600 | tf_op jit(solution)/shard_map/reshape | solution.py:251
  770.6 721.9 %all-reduce.3.cloned.1.call-done = f32[32,393600]{1,0:T(8,128)} async-done(((f32[32,393600]{1,0:T(8,128)}), f32[32,393600]{1,0:T(8,128)}) %all-reduce.3.cloned.1.call-update) | async-done | bytes 50380816
  1492.5 5.5 constant_dynamic-slice_fusion
  1499.1 3.4 collective-permute-start.1
  1502.5 18.2 collective-permute-done
  1520.7 13.2 collective-permute-start.2
  1533.9 9.4 collective-permute-done.2
  1543.4 26.2 %collective-permute-start.4 = (f32[1,393600]{1,0:T(1,128)S(1)}, f32[1,393600]{1,0:T(1,128)S(1)}, u32[]{:S(2)}, u32[]{:S(2)}) collective-permute-start(f32[1,393600]{1,0:T(1,128)S(1)} %collective-permute-done.2), channel_id=1, source_target_pairs={{0,2},{2,4},{4,6},{6,8},{8,10},{10,12},{12,14},{14,16},{16,18},{18... | collective-permute-start | bytes 4723208 | tf_op jit(solution)/shard_map/ppermute | solution.py:24
  1572.6 32.9 %collective-permute-start.6 = (f32[1,393600]{1,0:T(1,128)S(1)}, f32[1,393600]{1,0:T(1,128)S(1)}, u32[]{:S(2)}, u32[]{:S(2)}) collective-permute-start(f32[1,393600]{1,0:T(1,128)S(1)} %collective-permute-done.4), channel_id=1, source_target_pairs={{0,2},{2,4},{4,6},{6,8},{8,10},{10,12},{12,14},{14,16},{16,18},{18... | collective-permute-start | bytes 4723208 | tf_op jit(solution)/shard_map/ppermute | solution.py:24
  1608.6 32.0 %collective-permute-start.8 = (f32[1,393600]{1,0:T(1,128)S(1)}, f32[1,393600]{1,0:T(1,128)S(1)}, u32[]{:S(2)}, u32[]{:S(2)}) collective-permute-start(f32[1,393600]{1,0:T(1,128)S(1)} %collective-permute-done.6), channel_id=1, source_target_pairs={{0,2},{2,4},{4,6},{6,8},{8,10},{10,12},{12,14},{14,16},{16,18},{18... | collective-permute-start | bytes 4723208 | tf_op jit(solution)/shard_map/ppermute | solution.py:24
  1643.6 33.0 %collective-permute-start.10 = (f32[1,393600]{1,0:T(1,128)S(1)}, f32[1,393600]{1,0:T(1,128)}, u32[]{:S(2)}, u32[]{:S(2)}) collective-permute-start(f32[1,393600]{1,0:T(1,128)S(1)} %collective-permute-done.8), channel_id=1, source_target_pairs={{0,2},{2,4},{4,6},{6,8},{8,10},{10,12},{12,14},{14,16},{16,18},{18... | collective-permute-start | bytes 4723208 | tf_op jit(solution)/shard_map/ppermute | solution.py:24
  1676.6 3.2 collective-permute-done.10
  1679.8 32.7 %collective-permute-start.12 = (f32[1,393600]{1,0:T(1,128)}, f32[1,393600]{1,0:T(1,128)}, u32[]{:S(2)}, u32[]{:S(2)}) collective-permute-start(f32[1,393600]{1,0:T(1,128)} %collective-permute-done.10), channel_id=1, source_target_pairs={{0,2},{2,4},{4,6},{6,8},{8,10},{10,12},{12,14},{14,16},{16,18},{18... | collective-permute-start | bytes 4723208 | tf_op jit(solution)/shard_map/ppermute | solution.py:24
  1715.8 34.0 %collective-permute-start.14 = (f32[1,393600]{1,0:T(1,128)}, f32[1,393600]{1,0:T(1,128)}, u32[]{:S(2)}, u32[]{:S(2)}) collective-permute-start(f32[1,393600]{1,0:T(1,128)} %collective-permute-done.12), channel_id=1, source_target_pairs={{0,2},{2,4},{4,6},{6,8},{8,10},{10,12},{12,14},{14,16},{16,18},{18... | collective-permute-start | bytes 4723208 | tf_op jit(solution)/shard_map/ppermute | solution.py:24
  1750.7 5.1 fusion.30
  1755.8 5.0 fusion.29
  1761.6 8.7 broadcast_in_dim.31
  1770.3 30.4 %dynamic_update_slice.48 = f32[16,393600]{1,0:T(8,128)} dynamic-update-slice(f32[16,393600]{1,0:T(8,128)} %broadcast_in_dim.31, f32[1,393600]{1,0:T(1,128)S(1)} %copy-done.26, s32[]{:T(128)S(6)} %select_n.122, s32[]{:T(128)} %constant.138.clone.1) | dynamic-update-slice | bytes 3148804 | tf_op jit(solution)/shard_map/dynamic_update_slice | solution.py:19
  1800.7 30.4 %dynamic_update_slice.49 = f32[16,393600]{1,0:T(8,128)} dynamic-update-slice(f32[16,393600]{1,0:T(8,128)} %dynamic_update_slice.48, f32[1,393600]{1,0:T(1,128)S(1)} %copy-done.48, s32[]{:T(128)S(6)} %select_n.124, s32[]{:T(128)} %constant.138.clone.1) | dynamic-update-slice | bytes 3148804 | tf_op jit(solution)/shard_map/dynamic_update_slice | solution.py:25
  1831.1 30.4 %dynamic_update_slice.50 = f32[16,393600]{1,0:T(8,128)} dynamic-update-slice(f32[16,393600]{1,0:T(8,128)} %dynamic_update_slice.49, f32[1,393600]{1,0:T(1,128)S(1)} %copy-done.50, s32[]{:T(128)S(6)} %select_n.126, s32[]{:T(128)} %constant.138.clone.1) | dynamic-update-slice | bytes 3148804 | tf_op jit(solution)/shard_map/dynamic_update_slice | solution.py:28
  1861.5 30.4 %dynamic_update_slice.51 = f32[16,393600]{1,0:T(8,128)} dynamic-update-slice(f32[16,393600]{1,0:T(8,128)} %dynamic_update_slice.50, f32[1,393600]{1,0:T(1,128)S(1)} %copy-done.52, s32[]{:T(128)S(6)} %select_n.128, s32[]{:T(128)} %constant.138.clone.1) | dynamic-update-slice | bytes 3148804 | tf_op jit(solution)/shard_map/dynamic_update_slice | solution.py:25
  1891.9 30.4 %dynamic_update_slice.52 = f32[16,393600]{1,0:T(8,128)} dynamic-update-slice(f32[16,393600]{1,0:T(8,128)} %dynamic_update_slice.51, f32[1,393600]{1,0:T(1,128)S(1)} %copy-done.54, s32[]{:T(128)S(6)} %select_n.130, s32[]{:T(128)} %constant.138.clone.1) | dynamic-update-slice | bytes 3148804 | tf_op jit(solution)/shard_map/dynamic_update_slice | solution.py:28
  1922.2 30.4 %dynamic_update_slice.53 = f32[16,393600]{1,0:T(8,128)} dynamic-update-slice(f32[16,393600]{1,0:T(8,128)} %dynamic_update_slice.52, f32[1,393600]{1,0:T(1,128)S(1)} %copy-done.56, s32[]{:T(128)S(6)} %select_n.132, s32[]{:T(128)} %constant.138.clone.1) | dynamic-update-slice | bytes 3148804 | tf_op jit(solution)/shard_map/dynamic_update_slice | solution.py:25
  1952.6 30.4 %dynamic_update_slice.54 = f32[16,393600]{1,0:T(8,128)} dynamic-update-slice(f32[16,393600]{1,0:T(8,128)} %dynamic_update_slice.53, f32[1,393600]{1,0:T(1,128)S(1)} %copy-done.58, s32[]{:T(128)S(6)} %select_n.134, s32[]{:T(128)} %constant.138.clone.1) | dynamic-update-slice | bytes 3148804 | tf_op jit(solution)/shard_map/dynamic_update_slice | solution.py:28
  1983.0 30.4 %dynamic_update_slice.55 = f32[16,393600]{1,0:T(8,128)} dynamic-update-slice(f32[16,393600]{1,0:T(8,128)} %dynamic_update_slice.54, f32[1,393600]{1,0:T(1,128)S(1)} %copy-done.60, s32[]{:T(128)S(6)} %select_n.136, s32[]{:T(128)} %constant.138.clone.1) | dynamic-update-slice | bytes 3148804 | tf_op jit(solution)/shard_map/dynamic_update_slice | solution.py:25
  2013.4 30.4 %dynamic_update_slice.56 = f32[16,393600]{1,0:T(8,128)} dynamic-update-slice(f32[16,393600]{1,0:T(8,128)} %dynamic_update_slice.55, f32[1,393600]{1,0:T(1,128)S(1)} %copy-done.62, s32[]{:T(128)S(6)} %select_n.138, s32[]{:T(128)} %constant.138.clone.1) | dynamic-update-slice | bytes 3148804 | tf_op jit(solution)/shard_map/dynamic_update_slice | solution.py:28
  2043.8 30.3 %dynamic_update_slice.57 = f32[16,393600]{1,0:T(8,128)} dynamic-update-slice(f32[16,393600]{1,0:T(8,128)} %dynamic_update_slice.56, f32[1,393600]{1,0:T(1,128)S(1)} %copy-done.64, s32[]{:T(128)S(6)} %select_n.140, s32[]{:T(128)} %constant.138.clone.1) | dynamic-update-slice | bytes 3148804 | tf_op jit(solution)/shard_map/dynamic_update_slice | solution.py:25
  2074.0 30.4 %dynamic_update_slice.58 = f32[16,393600]{1,0:T(8,128)} dynamic-update-slice(f32[16,393600]{1,0:T(8,128)} %dynamic_update_slice.57, f32[1,393600]{1,0:T(1,128)} %collective-permute-done.9, s32[]{:T(128)S(6)} %select_n.142, s32[]{:T(128)} %constant.138.clone.1) | dynamic-update-slice | bytes 3148804 | tf_op jit(solution)/shard_map/dynamic_update_slice | solution.py:28
  2104.4 30.4 %dynamic_update_slice.59 = f32[16,393600]{1,0:T(8,128)} dynamic-update-slice(f32[16,393600]{1,0:T(8,128)} %dynamic_update_slice.58, f32[1,393600]{1,0:T(1,128)} %collective-permute-done.10, s32[]{:T(128)S(6)} %select_n.144, s32[]{:T(128)} %constant.138.clone.1) | dynamic-update-slice | bytes 3148804 | tf_op jit(solution)/shard_map/dynamic_update_slice | solution.py:25
  2134.8 30.4 %dynamic_update_slice.60 = f32[16,393600]{1,0:T(8,128)} dynamic-update-slice(f32[16,393600]{1,0:T(8,128)} %dynamic_update_slice.59, f32[1,393600]{1,0:T(1,128)} %collective-permute-done.11, s32[]{:T(128)S(6)} %select_n.146, s32[]{:T(128)} %constant.138.clone.1) | dynamic-update-slice | bytes 3148804 | tf_op jit(solution)/shard_map/dynamic_update_slice | solution.py:28
  2165.2 30.4 %dynamic_update_slice.61 = f32[16,393600]{1,0:T(8,128)} dynamic-update-slice(f32[16,393600]{1,0:T(8,128)} %dynamic_update_slice.60, f32[1,393600]{1,0:T(1,128)} %collective-permute-done.12, s32[]{:T(128)S(6)} %select_n.148, s32[]{:T(128)} %constant.138.clone.1) | dynamic-update-slice | bytes 3148804 | tf_op jit(solution)/shard_map/dynamic_update_slice | solution.py:25
  2195.6 30.4 %dynamic_update_slice.62 = f32[16,393600]{1,0:T(8,128)} dynamic-update-slice(f32[16,393600]{1,0:T(8,128)} %dynamic_update_slice.61, f32[1,393600]{1,0:T(1,128)} %collective-permute-done.13, s32[]{:T(128)S(6)} %select_n.150, s32[]{:T(128)} %constant.138.clone.1) | dynamic-update-slice | bytes 3148804 | tf_op jit(solution)/shard_map/dynamic_update_slice | solution.py:28
  2226.0 30.4 %dynamic_update_slice.63 = f32[16,393600]{1,0:T(8,128)} dynamic-update-slice(f32[16,393600]{1,0:T(8,128)} %dynamic_update_slice.62, f32[1,393600]{1,0:T(1,128)} %collective-permute-done.14, s32[]{:T(128)S(6)} %select_n.152, s32[]{:T(128)} %constant.138.clone.1) | dynamic-update-slice | bytes 3148804 | tf_op jit(solution)/shard_map/dynamic_update_slice | solution.py:25
  2256.4 20.3 reshape.379
  2276.7 61.2 %fusion.103 = (bf16[6297600]{0:T(1024)(128)(2,1)}, f32[6297600]{0:T(1024)}, f32[6297600]{0:T(1024)}, f32[6297600]{0:T(1024)}) fusion(s32[]{:T(128)S(6)} %mul.433, bf16[6297600]{0:T(1024)(128)(2,1)} %param.7, f32[6297600]{0:T(1024)} %reshape.379, f32[6297600]{0:T(1024)} %param.9, f32[6297600]{0:T(1024)} %param.8), kind=kLoop, calls=%fused_computation.218 | loop fusion | flops 107059200 | bytes 176332800 | tf_op jit(solution)/shard_map/convert_element_type | solution.py:272
  (362 shorter events, 81.8 us)
Async XLA Ops:
  7.2 301.6 %all-gather.2.cloned.1.call-start = ((), (), s32[]{:S(2)}) async-start(), calls=%async_computation | async-start | bytes 37785600 | tf_op jit(solution)/shard_map/all_gather | solution.py:224
  7.9 1484.5 %all-reduce.3.cloned.1.call-start = ((), (), s32[]{:S(2)}) async-start(), calls=%async_computation.1 | async-start | bytes 100761600
  8.7 318.1 %copy-start.82 = (f32[128]{0:T(128)}, f32[128]{0:T(128)S(1)}, u32[]{:S(2)}) copy-start(f32[128]{0:T(128)S(1)} %get-tuple-element.90) | copy-start | bytes 1540
  8.7 391.1 %copy-start.78 = (f32[128]{0:T(128)}, f32[128]{0:T(128)S(1)}, u32[]{:S(2)}) copy-start(f32[128]{0:T(128)S(1)} %get-tuple-element.89) | copy-start | bytes 1540
  9.0 317.7 %copy-start.86 = (f32[128]{0:T(128)}, f32[128]{0:T(128)S(1)}, u32[]{:S(2)}) copy-start(f32[128]{0:T(128)S(1)} %add_rsqrt_fusion.3) | copy-start | bytes 1540
  9.1 390.8 %copy-start.90 = (f32[128]{0:T(128)}, f32[128]{0:T(128)S(1)}, u32[]{:S(2)}) copy-start(f32[128]{0:T(128)S(1)} %add_rsqrt_fusion.1) | copy-start | bytes 1540
  380.9 18.9 slice-start.16
  386.9 13.0 slice-start.17
  413.1 15.7 copy-start.2
  442.9 14.6 slice-start.2
  466.6 14.3 copy-start.12
  466.6 14.3 copy-start.23
  466.6 14.3 copy-start.41
  512.1 10.4 copy-start.10
  530.9 18.7 slice-start.6
  530.9 18.7 slice-start.7
  530.9 18.7 slice-start.8
  547.1 10.9 slice-start.10
  549.6 10.8 slice-start.13
  560.5 10.3 copy-start.76
  560.5 10.3 copy-start.77
  560.5 10.9 copy-start.68
  560.5 10.9 copy-start.69
  770.5 942.0 %copy-start.104 = (f32[128]{0:T(128)S(1)}, f32[128]{0:T(128)}, u32[]{:S(2)}) copy-start(f32[128]{0:T(128)} %get-tuple-element.15) | copy-start | bytes 1540
  770.5 942.0 %copy-start.103 = (f32[128]{0:T(128)S(1)}, f32[128]{0:T(128)}, u32[]{:S(2)}) copy-start(f32[128]{0:T(128)} %get-tuple-element.17) | copy-start | bytes 1540
  770.5 942.0 %copy-start.102 = (f32[128]{0:T(128)S(1)}, f32[128]{0:T(128)}, u32[]{:S(2)}) copy-start(f32[128]{0:T(128)} %get-tuple-element.14) | copy-start | bytes 1540
  770.5 942.0 %copy-start.101 = (f32[128]{0:T(128)S(1)}, f32[128]{0:T(128)}, u32[]{:S(2)}) copy-start(f32[128]{0:T(128)} %get-tuple-element.18) | copy-start | bytes 1540
  770.5 942.0 %copy-start.17 = (bf16[2,128,1024]{2,1,0:T(8,128)(2,1)S(1)}, bf16[2,128,1024]{2,1,0:T(8,128)(2,1)}, u32[]{:S(2)}) copy-start(bf16[2,128,1024]{2,1,0:T(8,128)(2,1)} %param.10) | copy-start | bytes 1572868
  770.5 942.0 %copy-start.81 = (f32[128]{0:T(128)S(1)}, f32[128]{0:T(128)}, u32[]{:S(2)}) copy-start(f32[128]{0:T(128)} %copy-done.78) | copy-start | bytes 1540
  770.5 942.0 %copy-start.85 = (f32[128]{0:T(128)S(1)}, f32[128]{0:T(128)}, u32[]{:S(2)}) copy-start(f32[128]{0:T(128)} %copy-done.82) | copy-start | bytes 1540
  770.5 942.0 %copy-start.89 = (f32[128]{0:T(128)S(1)}, f32[128]{0:T(128)}, u32[]{:S(2)}) copy-start(f32[128]{0:T(128)} %copy-done.86) | copy-start | bytes 1540
  770.5 942.0 %copy-start.93 = (f32[128]{0:T(128)S(1)}, f32[128]{0:T(128)}, u32[]{:S(2)}) copy-start(f32[128]{0:T(128)} %copy-done.90) | copy-start | bytes 1540
  770.5 980.1 %copy-start.8 = (f32[128,1024]{1,0:T(8,128)S(1)}, f32[128,1024]{1,0:T(8,128)}, u32[]{:S(2)}) copy-start(f32[128,1024]{1,0:T(8,128)} %copy-done.5) | copy-start | bytes 1572868
  770.6 980.1 %copy-start.20 = (f32[128,4096]{1,0:T(8,128)S(1)}, f32[128,4096]{1,0:T(8,128)}, u32[]{:S(2)}) copy-start(f32[128,4096]{1,0:T(8,128)} %copy-done.18) | copy-start | bytes 6291460
  770.6 980.1 %copy-start.98 = (f32[1024]{0:T(1024)S(1)}, f32[1024]{0:T(1024)}, u32[]{:S(2)}) copy-start(f32[1024]{0:T(1024)} %get-tuple-element.40) | copy-start | bytes 12292
  1498.0 22.7 collective-permute-start
  1499.1 34.8 %collective-permute-start.1 = (f32[1,393600]{1,0:T(1,128)S(1)}, f32[1,393600]{1,0:T(1,128)S(1)}, u32[]{:S(2)}, u32[]{:S(2)}) collective-permute-start(f32[1,393600]{1,0:T(1,128)S(1)} %constant_dynamic-slice_fusion), channel_id=1, source_target_pairs={{0,30},{2,0},{4,2},{6,4},{8,6},{10,8},{12,10},{14,12},{16,14},{18,... | collective-permute-start | bytes 4723208 | tf_op jit(solution)/shard_map/ppermute | solution.py:27
  1520.7 13.2 copy-start.47
  1520.7 22.7 collective-permute-start.2
  1533.9 35.7 %collective-permute-start.3 = (f32[1,393600]{1,0:T(1,128)S(1)}, f32[1,393600]{1,0:T(1,128)S(1)}, u32[]{:S(2)}, u32[]{:S(2)}) collective-permute-start(f32[1,393600]{1,0:T(1,128)S(1)} %collective-permute-done.1), channel_id=1, source_target_pairs={{0,30},{2,0},{4,2},{6,4},{8,6},{10,8},{12,10},{14,12},{16,14},{18,... | collective-permute-start | bytes 4723208 | tf_op jit(solution)/shard_map/ppermute | solution.py:27
  1543.4 26.2 %copy-start.51 = (f32[1,393600]{1,0:T(1,128)}, f32[1,393600]{1,0:T(1,128)S(1)}, u32[]{:S(2)}) copy-start(f32[1,393600]{1,0:T(1,128)S(1)} %collective-permute-done.2) | copy-start | bytes 4723204
  1543.4 29.3 %collective-permute-start.4 = (f32[1,393600]{1,0:T(1,128)S(1)}, f32[1,393600]{1,0:T(1,128)S(1)}, u32[]{:S(2)}, u32[]{:S(2)}) collective-permute-start(f32[1,393600]{1,0:T(1,128)S(1)} %collective-permute-done.2), channel_id=1, source_target_pairs={{0,2},{2,4},{4,6},{6,8},{8,10},{10,12},{12,14},{14,16},{16,18},{18... | collective-permute-start | bytes 4723208 | tf_op jit(solution)/shard_map/ppermute | solution.py:24
  1569.6 35.9 %collective-permute-start.5 = (f32[1,393600]{1,0:T(1,128)S(1)}, f32[1,393600]{1,0:T(1,128)S(1)}, u32[]{:S(2)}, u32[]{:S(2)}) collective-permute-start(f32[1,393600]{1,0:T(1,128)S(1)} %collective-permute-done.3), channel_id=1, source_target_pairs={{0,30},{2,0},{4,2},{6,4},{8,6},{10,8},{12,10},{14,12},{16,14},{18,... | collective-permute-start | bytes 4723208 | tf_op jit(solution)/shard_map/ppermute | solution.py:27
  1572.6 32.9 %copy-start.55 = (f32[1,393600]{1,0:T(1,128)}, f32[1,393600]{1,0:T(1,128)S(1)}, u32[]{:S(2)}) copy-start(f32[1,393600]{1,0:T(1,128)S(1)} %collective-permute-done.4) | copy-start | bytes 4723204
  1572.6 35.9 %collective-permute-start.6 = (f32[1,393600]{1,0:T(1,128)S(1)}, f32[1,393600]{1,0:T(1,128)S(1)}, u32[]{:S(2)}, u32[]{:S(2)}) collective-permute-start(f32[1,393600]{1,0:T(1,128)S(1)} %collective-permute-done.4), channel_id=1, source_target_pairs={{0,2},{2,4},{4,6},{6,8},{8,10},{10,12},{12,14},{14,16},{16,18},{18... | collective-permute-start | bytes 4723208 | tf_op jit(solution)/shard_map/ppermute | solution.py:24
  1605.5 35.1 %collective-permute-start.7 = (f32[1,393600]{1,0:T(1,128)S(1)}, f32[1,393600]{1,0:T(1,128)S(1)}, u32[]{:S(2)}, u32[]{:S(2)}) collective-permute-start(f32[1,393600]{1,0:T(1,128)S(1)} %collective-permute-done.5), channel_id=1, source_target_pairs={{0,30},{2,0},{4,2},{6,4},{8,6},{10,8},{12,10},{14,12},{16,14},{18,... | collective-permute-start | bytes 4723208 | tf_op jit(solution)/shard_map/ppermute | solution.py:27
  1608.5 32.0 %copy-start.59 = (f32[1,393600]{1,0:T(1,128)}, f32[1,393600]{1,0:T(1,128)S(1)}, u32[]{:S(2)}) copy-start(f32[1,393600]{1,0:T(1,128)S(1)} %collective-permute-done.6) | copy-start | bytes 4723204
  1608.6 35.1 %collective-permute-start.8 = (f32[1,393600]{1,0:T(1,128)S(1)}, f32[1,393600]{1,0:T(1,128)S(1)}, u32[]{:S(2)}, u32[]{:S(2)}) collective-permute-start(f32[1,393600]{1,0:T(1,128)S(1)} %collective-permute-done.6), channel_id=1, source_target_pairs={{0,2},{2,4},{4,6},{6,8},{8,10},{10,12},{12,14},{14,16},{16,18},{18... | collective-permute-start | bytes 4723208 | tf_op jit(solution)/shard_map/ppermute | solution.py:24
  1640.6 36.0 %collective-permute-start.9 = (f32[1,393600]{1,0:T(1,128)S(1)}, f32[1,393600]{1,0:T(1,128)}, u32[]{:S(2)}, u32[]{:S(2)}) collective-permute-start(f32[1,393600]{1,0:T(1,128)S(1)} %collective-permute-done.7), channel_id=1, source_target_pairs={{0,30},{2,0},{4,2},{6,4},{8,6},{10,8},{12,10},{14,12},{16,14},{18,... | collective-permute-start | bytes 4723208 | tf_op jit(solution)/shard_map/ppermute | solution.py:27
  1643.6 33.0 %copy-start.63 = (f32[1,393600]{1,0:T(1,128)}, f32[1,393600]{1,0:T(1,128)S(1)}, u32[]{:S(2)}) copy-start(f32[1,393600]{1,0:T(1,128)S(1)} %collective-permute-done.8) | copy-start | bytes 4723204
  1643.6 36.1 %collective-permute-start.10 = (f32[1,393600]{1,0:T(1,128)S(1)}, f32[1,393600]{1,0:T(1,128)}, u32[]{:S(2)}, u32[]{:S(2)}) collective-permute-start(f32[1,393600]{1,0:T(1,128)S(1)} %collective-permute-done.8), channel_id=1, source_target_pairs={{0,2},{2,4},{4,6},{6,8},{8,10},{10,12},{12,14},{14,16},{16,18},{18... | collective-permute-start | bytes 4723208 | tf_op jit(solution)/shard_map/ppermute | solution.py:24
  1676.6 37.9 %collective-permute-start.11 = (f32[1,393600]{1,0:T(1,128)}, f32[1,393600]{1,0:T(1,128)}, u32[]{:S(2)}, u32[]{:S(2)}) collective-permute-start(f32[1,393600]{1,0:T(1,128)} %collective-permute-done.9), channel_id=1, source_target_pairs={{0,30},{2,0},{4,2},{6,4},{8,6},{10,8},{12,10},{14,12},{16,14},{18,... | collective-permute-start | bytes 4723208 | tf_op jit(solution)/shard_map/ppermute | solution.py:27
  1679.8 36.1 %collective-permute-start.12 = (f32[1,393600]{1,0:T(1,128)}, f32[1,393600]{1,0:T(1,128)}, u32[]{:S(2)}, u32[]{:S(2)}) collective-permute-start(f32[1,393600]{1,0:T(1,128)} %collective-permute-done.10), channel_id=1, source_target_pairs={{0,2},{2,4},{4,6},{6,8},{8,10},{10,12},{12,14},{14,16},{16,18},{18... | collective-permute-start | bytes 4723208 | tf_op jit(solution)/shard_map/ppermute | solution.py:24
  1714.5 481.1 %collective-permute-start.13 = (f32[1,393600]{1,0:T(1,128)}, f32[1,393600]{1,0:T(1,128)}, u32[]{:S(2)}, u32[]{:S(2)}) collective-permute-start(f32[1,393600]{1,0:T(1,128)} %collective-permute-done.11), channel_id=1, source_target_pairs={{0,30},{2,0},{4,2},{6,4},{8,6},{10,8},{12,10},{14,12},{16,14},{18,... | collective-permute-start | bytes 4723208 | tf_op jit(solution)/shard_map/ppermute | solution.py:27
  1715.8 510.1 %collective-permute-start.14 = (f32[1,393600]{1,0:T(1,128)}, f32[1,393600]{1,0:T(1,128)}, u32[]{:S(2)}, u32[]{:S(2)}) collective-permute-start(f32[1,393600]{1,0:T(1,128)} %collective-permute-done.12), channel_id=1, source_target_pairs={{0,2},{2,4},{4,6},{6,8},{8,10},{10,12},{12,14},{14,16},{16,18},{18... | collective-permute-start | bytes 4723208 | tf_op jit(solution)/shard_map/ppermute | solution.py:24
  1770.3 30.4 %copy-start.48 = (f32[1,393600]{1,0:T(1,128)S(1)}, f32[1,393600]{1,0:T(1,128)}, u32[]{:S(2)}) copy-start(f32[1,393600]{1,0:T(1,128)} %copy-done.47) | copy-start | bytes 4723204
  1800.7 30.4 %copy-start.50 = (f32[1,393600]{1,0:T(1,128)S(1)}, f32[1,393600]{1,0:T(1,128)}, u32[]{:S(2)}) copy-start(f32[1,393600]{1,0:T(1,128)} %copy-done.49) | copy-start | bytes 4723204
  1831.1 30.4 %copy-start.52 = (f32[1,393600]{1,0:T(1,128)S(1)}, f32[1,393600]{1,0:T(1,128)}, u32[]{:S(2)}) copy-start(f32[1,393600]{1,0:T(1,128)} %copy-done.51) | copy-start | bytes 4723204
  1861.5 30.4 %copy-start.54 = (f32[1,393600]{1,0:T(1,128)S(1)}, f32[1,393600]{1,0:T(1,128)}, u32[]{:S(2)}) copy-start(f32[1,393600]{1,0:T(1,128)} %copy-done.53) | copy-start | bytes 4723204
  1891.9 30.4 %copy-start.56 = (f32[1,393600]{1,0:T(1,128)S(1)}, f32[1,393600]{1,0:T(1,128)}, u32[]{:S(2)}) copy-start(f32[1,393600]{1,0:T(1,128)} %copy-done.55) | copy-start | bytes 4723204
  1922.2 30.4 %copy-start.58 = (f32[1,393600]{1,0:T(1,128)S(1)}, f32[1,393600]{1,0:T(1,128)}, u32[]{:S(2)}) copy-start(f32[1,393600]{1,0:T(1,128)} %copy-done.57) | copy-start | bytes 4723204
  1952.6 30.4 %copy-start.60 = (f32[1,393600]{1,0:T(1,128)S(1)}, f32[1,393600]{1,0:T(1,128)}, u32[]{:S(2)}) copy-start(f32[1,393600]{1,0:T(1,128)} %copy-done.59) | copy-start | bytes 4723204
  1983.0 30.4 %copy-start.62 = (f32[1,393600]{1,0:T(1,128)S(1)}, f32[1,393600]{1,0:T(1,128)}, u32[]{:S(2)}) copy-start(f32[1,393600]{1,0:T(1,128)} %copy-done.61) | copy-start | bytes 4723204
  2013.4 30.4 %copy-start.64 = (f32[1,393600]{1,0:T(1,128)S(1)}, f32[1,393600]{1,0:T(1,128)}, u32[]{:S(2)}) copy-start(f32[1,393600]{1,0:T(1,128)} %copy-done.63) | copy-start | bytes 4723204
  (78 other events, 457.7 us)
Sparse Core Ops, SparseCore 0:
  9.6 299.1 all-gather.1
  770.7 721.7 all-reduce.2
